TPU v7x, 512 devices: a whole 4x8x8 slice. The times are simulated.
512 devices in a mesh: layer: 32 (over x_lo, y, core), tp: 16 (over z, x_hi).
Axes of the slice: x: 4 (x_hi: 2, x_lo: 2; x = x_hi * 2 + x_lo), y: 8, z: 8, core: 2. Of those that a mesh axis runs over, the one named last changes fastest.
Arguments:
- acts: bfloat16 [4096, 2048], P(('layer', 'tp')), may hold values from -12 to 12, as said below
- fresh: bfloat16 [2, 128, 2048], P(None, 'tp'), may hold values from -12 to 12, as said below
- norm_first: float32 [16, 2048], replicated, may hold values from 0.5 to 1.5
- norm_second: float32 [16, 2048], replicated, may hold values from 0.5 to 1.5
- proj_qkv: bfloat16 [512, 2048, 192], P(('layer', 'tp')), may hold values from -1 to 1
- proj_out: bfloat16 [32768, 2048], P(('layer', 'tp')), may hold values from -0.125 to 0.125
- proj_gate_up: bfloat16 [2048, 2, 131072], P(None, None, ('layer', 'tp')), may hold values from -0.125 to 0.125
- proj_down: bfloat16 [131072, 2048], P(('layer', 'tp')), may hold values from -0.0625 to 0.0625
- memory_state: float32 [512, 64, 64], P(('layer', 'tp')), may hold values from -768 to 768
- memory_norm: float32 [512, 64], P(('layer', 'tp')), may hold values from 16 to 256
- bias_gate: float32 [512], P(('layer', 'tp')), may hold values from -3 to 3
Outputs:
- first_out: bfloat16 [4096, 2048], P(('layer', 'tp'))
- second_out: bfloat16 [4096, 2048], P(('layer', 'tp'))
- memory_after: float32 [512, 64, 64], P(('layer', 'tp'))
- norm_after: float32 [512, 64], P(('layer', 'tp'))
Inputs may be any that keep to these rules, and one draw needn't show every extreme that they name: `acts`: activation rows. `fresh`: activation rows.
All inputs are finite; a program needn't handle non-finite values.
Results may differ from a plain program's by a relative error of at most 0.025.
Values may be sent and summed in bfloat16 or wider, within the bound.
No kernel may reach another device: no remote copies, remote signals or barrier semaphores. Data moves between devices by JAX's collectives and lax.ppermute only.
A program may use at most 64 MiB of HBM per device.

v0:
```python
import jax
import jax.numpy as jnp
from jax import lax
from jax.sharding import PartitionSpec as P


def partner_2(value, axis, distance):
    mask = 2**distance
    pairs = [(source, source ^ mask) for source in range(lax.axis_size(axis))]
    return lax.ppermute(value, axis, pairs)


def shifted(value, axis, steps):
    count = lax.axis_size(axis)
    initial, last = (max(0, -steps), min(count, count - steps))
    return lax.ppermute(value, axis, [(source, source + steps) for source in range(initial, last)])


def rms_norm(values, weight):
    floats = values.astype(jnp.float32)
    scaled = floats * lax.rsqrt(jnp.mean(floats * floats, axis=-1, keepdims=True) + 1e-05)
    return (scaled * weight).astype(jnp.bfloat16)


def attend(qkv, memory, totals, logits):
    head_dim = memory.shape[-1]
    seg_len = qkv.shape[0]
    queries = qkv[..., :head_dim]
    keyed = qkv[..., head_dim : 2 * head_dim]
    valued = qkv[..., 2 * head_dim :]
    scores = jnp.einsum(
        "qhc,khc->hqk", queries, keyed, preferred_element_type=jnp.float32
    ) * head_dim ** (-0.5)
    positions = jnp.arange(seg_len)
    allowed = positions[:, None] >= positions[None, :]
    probs = jax.nn.softmax(jnp.where(allowed[None], scores, -jnp.inf), axis=-1).astype(jnp.bfloat16)
    direct = jnp.einsum("hqk,khc->qhc", probs, valued, preferred_element_type=jnp.float32)
    lifted_q = jax.nn.elu(queries.astype(jnp.float32)) + 1.0
    lifted_k = jax.nn.elu(keyed.astype(jnp.float32)) + 1.0
    numer = jnp.einsum("qhc,hce->qhe", lifted_q, memory, precision=lax.Precision.HIGHEST)
    denom = jnp.einsum("qhc,hc->qh", lifted_q, totals, precision=lax.Precision.HIGHEST)[..., None]
    gate_open = jax.nn.sigmoid(logits)[None, :, None]
    blended = (gate_open * numer / denom + (1.0 - gate_open) * direct).astype(jnp.bfloat16)
    new_memory = memory + jnp.einsum(
        "khc,khe->hce", lifted_k, valued.astype(jnp.float32), precision=lax.Precision.HIGHEST
    )
    new_totals = totals + jnp.sum(lifted_k, axis=0)
    return (blended.reshape(seg_len, -1), new_memory, new_totals)


def body(
    acts,
    fresh,
    norm_first,
    norm_second,
    proj_qkv,
    proj_out,
    proj_gate_up,
    proj_down,
    memory_state,
    memory_norm,
    bias_gate,
):
    position = lax.axis_index("layer")
    lower = position % 2 == 0
    depth = position // 2
    member = lax.axis_index("tp")
    gain_one = lax.dynamic_index_in_dim(norm_first, depth, 0, keepdims=False)
    gain_two = lax.dynamic_index_in_dim(norm_second, depth, 0, keepdims=False)
    row_count = acts.shape[0]

    def ordered(mine, other):
        return jnp.concatenate(
            [jnp.where(lower, mine, other), jnp.where(lower, other, mine)], axis=0
        )

    def project(rows):
        return jnp.einsum("sd,hdc->shc", rows, proj_qkv, preferred_element_type=jnp.float32).astype(
            jnp.bfloat16
        )

    def expand(rows):
        gate_up = jnp.einsum("sd,dtf->stf", rows, proj_gate_up, preferred_element_type=jnp.float32)
        return (jax.nn.silu(gate_up[:, 0]) * gate_up[:, 1]).astype(jnp.bfloat16)

    def collect_all(values):
        partner = partner_2(values, "layer", 0)
        mine, other = (
            lax.all_gather(values, "tp", axis=0, tiled=True),
            lax.all_gather(partner, "tp", axis=0, tiled=True),
        )
        return ordered(mine, other)

    def total_all(local, weight):
        summed = lax.psum(
            jnp.dot(local, weight, preferred_element_type=jnp.float32).astype(jnp.bfloat16), "tp"
        ).astype(jnp.float32)
        return summed + partner_2(summed.astype(jnp.bfloat16), "layer", 0).astype(summed.dtype)

    def apply_layer(stream, memory, totals):
        gathered = collect_all(stream)
        seg_len = gathered.shape[0]
        qkv = project(rms_norm(gathered, gain_one))
        blended, memory, totals = attend(qkv, memory, totals, bias_gate)
        attn = total_all(blended, proj_out)
        hidden_one = (gathered.astype(jnp.float32) + attn).astype(jnp.bfloat16)
        hidden = expand(rms_norm(hidden_one, gain_two))
        ffn = total_all(hidden, proj_down)
        complete = (hidden_one.astype(jnp.float32) + ffn).astype(jnp.bfloat16)
        start = position % 2 * (seg_len // 2) + member * row_count
        output = lax.dynamic_slice_in_dim(complete, start, row_count, 0)
        return (output, memory, totals)

    first_rows, memory_one, totals_one = apply_layer(acts, memory_state, memory_norm)
    incoming = shifted(first_rows, "layer", 2)
    fresh_rows = lax.dynamic_index_in_dim(fresh, position % 2, 0, keepdims=False)
    entering = jnp.where(depth == 0, fresh_rows, incoming)
    second_rows, memory_two, totals_two = apply_layer(entering, memory_one, totals_one)
    return (first_rows, second_rows, memory_two, totals_two)


def solution(mesh):
    in_specs = (
        P(("layer", "tp"), None),
        P(None, "tp", None),
        P(),
        P(),
        P(("layer", "tp"), None, None),
        P(("layer", "tp"), None),
        P(None, None, ("layer", "tp")),
        P(("layer", "tp"), None),
        P(("layer", "tp"), None, None),
        P(("layer", "tp"), None),
        P(("layer", "tp")),
    )
    out_specs = (
        P(("layer", "tp"), None),
        P(("layer", "tp"), None),
        P(("layer", "tp"), None, None),
        P(("layer", "tp"), None),
    )
    return jax.shard_map(body, mesh=mesh, in_specs=in_specs, out_specs=out_specs, check_vma=False)
```

profile of v0, /device:TPU:1, one launch (start us, length us, event | category | flops | bytes accessed | tf_op | source)
XLA Modules:
  0.0 903.9 jit_solution(7788227879883312457)
XLA Ops:
  7.2 8.9 collective-permute-start
  16.1 40.0 %all_gather.12 = bf16[128,2048]{1,0:T(8,128)(2,1)} all-gather(bf16[8,2048]{1,0:T(8,128)(2,1)} %param.11), channel_id=1, replica_groups=mesh['layer'=32,'tp'=16] {'tp'}, dimensions={0}, use_global_device_ids=true | all-gather | bytes 557056 | tf_op jit(solution)/shard_map/all_gather | solution.py:89
  57.7 31.6 %all_gather.13 = bf16[128,2048]{1,0:T(8,128)(2,1)S(1)} all-gather(bf16[8,2048]{1,0:T(8,128)(2,1)S(1)} %collective-permute-done), channel_id=1, replica_groups=mesh['layer'=32,'tp'=16] {'tp'}, dimensions={0}, use_global_device_ids=true | all-gather | bytes 557056 | tf_op jit(solution)/shard_map/all_gather | solution.py:90
  90.7 1.7 fusion.14
  93.3 2.7 convolution_convert_fusion.3
  96.1 167.5 %all-reduce.5.cloned.1.call-done = bf16[256,2048]{1,0:T(8,128)(2,1)} async-done(((bf16[256,2048]{1,0:T(8,128)(2,1)}), bf16[256,2048]{1,0:T(8,128)(2,1)}) %all-reduce.5.cloned.1.call-update) | async-done | bytes 1048592 | tf_op jit(solution)/shard_map/psum | solution.py:95
  263.6 13.1 %collective-permute-start.1 = (bf16[256,2048]{1,0:T(8,128)(2,1)}, bf16[256,2048]{1,0:T(8,128)(2,1)S(1)}, u32[]{:S(2)}, u32[]{:S(2)}) collective-permute-start(bf16[256,2048]{1,0:T(8,128)(2,1)} %all-reduce.5.cloned.1.call-done), channel_id=1, source_target_pairs={{0,16},{16,0},{32,48},{48,32},{64,80},{80,64},{96,112},{112,96},{1... | collective-permute-start | bytes 3145736 | tf_op jit(solution)/shard_map/ppermute | solution.py:10
  277.5 1.6 collective-permute-done.1
  279.2 1.8 multiply_reduce_fusion.1
  284.5 153.8 %all-reduce.7.cloned.1.call-done = bf16[256,2048]{1,0:T(8,128)(2,1)} async-done(((bf16[256,2048]{1,0:T(8,128)(2,1)}), bf16[256,2048]{1,0:T(8,128)(2,1)}) %all-reduce.7.cloned.1.call-update) | async-done | bytes 1048592 | tf_op jit(solution)/shard_map/psum | solution.py:95
  438.3 13.1 %collective-permute-start.2 = (bf16[256,2048]{1,0:T(8,128)(2,1)}, bf16[256,2048]{1,0:T(8,128)(2,1)S(1)}, u32[]{:S(2)}, u32[]{:S(2)}) collective-permute-start(bf16[256,2048]{1,0:T(8,128)(2,1)} %all-reduce.7.cloned.1.call-done), channel_id=1, source_target_pairs={{0,16},{16,0},{32,48},{48,32},{64,80},{80,64},{96,112},{112,96},{1... | collective-permute-start | bytes 3145736 | tf_op jit(solution)/shard_map/ppermute | solution.py:10
  451.7 2.2 collective-permute-done.2
  454.8 3.1 collective-permute-start.3
  458.9 3.3 collective-permute-start.4
  462.2 36.4 %all_gather.14 = bf16[128,2048]{1,0:T(8,128)(2,1)S(1)} all-gather(bf16[8,2048]{1,0:T(8,128)(2,1)S(1)} %bitcast_select_fusion), channel_id=1, replica_groups=mesh['layer'=32,'tp'=16] {'tp'}, dimensions={0}, use_global_device_ids=true | all-gather | bytes 557056 | tf_op jit(solution)/shard_map/all_gather | solution.py:89
  498.7 32.0 %all_gather.15 = bf16[128,2048]{1,0:T(8,128)(2,1)S(1)} all-gather(bf16[8,2048]{1,0:T(8,128)(2,1)S(1)} %collective-permute-done.4), channel_id=1, replica_groups=mesh['layer'=32,'tp'=16] {'tp'}, dimensions={0}, use_global_device_ids=true | all-gather | bytes 557056 | tf_op jit(solution)/shard_map/all_gather | solution.py:90
  532.6 2.6 convolution_convert_fusion.2
  535.3 170.2 %all-reduce.9.cloned.1.call-done = bf16[256,2048]{1,0:T(8,128)(2,1)} async-done(((bf16[256,2048]{1,0:T(8,128)(2,1)}), bf16[256,2048]{1,0:T(8,128)(2,1)}) %all-reduce.9.cloned.1.call-update) | async-done | bytes 1048592 | tf_op jit(solution)/shard_map/psum | solution.py:95
  705.5 13.1 %collective-permute-start.5 = (bf16[256,2048]{1,0:T(8,128)(2,1)}, bf16[256,2048]{1,0:T(8,128)(2,1)S(1)}, u32[]{:S(2)}, u32[]{:S(2)}) collective-permute-start(bf16[256,2048]{1,0:T(8,128)(2,1)} %all-reduce.9.cloned.1.call-done), channel_id=1, source_target_pairs={{0,16},{16,0},{32,48},{48,32},{64,80},{80,64},{96,112},{112,96},{1... | collective-permute-start | bytes 3145736 | tf_op jit(solution)/shard_map/ppermute | solution.py:10
  718.6 2.5 collective-permute-done.5
  721.0 1.8 multiply_reduce_fusion
  726.3 154.0 %all-reduce.11.cloned.1.call-done = bf16[256,2048]{1,0:T(8,128)(2,1)} async-done(((bf16[256,2048]{1,0:T(8,128)(2,1)}), bf16[256,2048]{1,0:T(8,128)(2,1)}) %all-reduce.11.cloned.1.call-update) | async-done | bytes 1048592 | tf_op jit(solution)/shard_map/psum | solution.py:95
  880.3 13.1 %collective-permute-start.6 = (bf16[256,2048]{1,0:T(8,128)(2,1)}, bf16[256,2048]{1,0:T(8,128)(2,1)S(1)}, u32[]{:S(2)}, u32[]{:S(2)}) collective-permute-start(bf16[256,2048]{1,0:T(8,128)(2,1)} %all-reduce.11.cloned.1.call-done), channel_id=1, source_target_pairs={{0,16},{16,0},{32,48},{48,32},{64,80},{80,64},{96,112},{112,96},{1... | collective-permute-start | bytes 3145736 | tf_op jit(solution)/shard_map/ppermute | solution.py:10
  895.9 1.5 fusion.76
  (76 shorter events, 17.6 us)
Async XLA Ops:
  7.2 273.8 %copy-start = (bf16[2048,2,256]{2,1,0:T(2,128)(2,1)S(1)}, bf16[2048,2,256]{2,1,0:T(2,128)(2,1)}, u32[]{:S(2)}) copy-start(bf16[2048,2,256]{2,1,0:T(2,128)(2,1)} %param.17) | copy-start | bytes 6291460
  7.2 256.4 %all-reduce.5.cloned.1.call-start = ((), (), s32[]{:S(2)}) async-start(), calls=%async_computation | async-start | bytes 2097152 | tf_op jit(solution)/shard_map/psum | solution.py:95
  7.2 50.5 %collective-permute-start = (bf16[8,2048]{1,0:T(8,128)(2,1)}, bf16[8,2048]{1,0:T(8,128)(2,1)S(1)}, u32[]{:S(2)}, u32[]{:S(2)}) collective-permute-start(bf16[8,2048]{1,0:T(8,128)(2,1)} %param.11), channel_id=1, source_target_pairs={{0,16},{16,0},{32,48},{48,32},{64,80},{80,64},{96,112},{112,96},{1... | collective-permute-start | bytes 98312 | tf_op jit(solution)/shard_map/ppermute | solution.py:10
  90.7 2.0 copy-start.9
  90.7 2.4 copy-start.13
  96.0 342.3 %all-reduce.7.cloned.1.call-start = ((), (), s32[]{:S(2)}) async-start(), calls=%async_computation.1 | async-start | bytes 2097152 | tf_op jit(solution)/shard_map/psum | solution.py:95
  263.6 15.6 %collective-permute-start.1 = (bf16[256,2048]{1,0:T(8,128)(2,1)}, bf16[256,2048]{1,0:T(8,128)(2,1)S(1)}, u32[]{:S(2)}, u32[]{:S(2)}) collective-permute-start(bf16[256,2048]{1,0:T(8,128)(2,1)} %all-reduce.5.cloned.1.call-done), channel_id=1, source_target_pairs={{0,16},{16,0},{32,48},{48,32},{64,80},{80,64},{96,112},{112,96},{1... | collective-permute-start | bytes 3145736 | tf_op jit(solution)/shard_map/ppermute | solution.py:10
  281.0 2.0 copy-start.10
  282.9 168.5 %copy-start.4 = (bf16[256,1,192]{0,2,1:T(8,128)(2,1)S(1)}, bf16[256,1,192]{0,2,1:T(8,128)(2,1)}, u32[]{:S(2)}) copy-start(bf16[256,1,192]{0,2,1:T(8,128)(2,1)} %copy-done.3) | copy-start | bytes 294916
  282.9 168.5 %copy-start.14 = (f32[1,64,64]{2,1,0:T(8,128)S(1)}, f32[1,64,64]{2,1,0:T(8,128)}, u32[]{:S(2)}) copy-start(f32[1,64,64]{2,1,0:T(8,128)} %param.19) | copy-start | bytes 49156
  283.0 176.0 %copy-start.8 = (bf16[2,8,2048]{2,1,0:T(8,128)(2,1)S(1)}, bf16[2,8,2048]{2,1,0:T(8,128)(2,1)}, u32[]{:S(2)}) copy-start(bf16[2,8,2048]{2,1,0:T(8,128)(2,1)} %param.12) | copy-start | bytes 196612
  284.4 421.0 %all-reduce.9.cloned.1.call-start = ((), (), s32[]{:S(2)}) async-start(), calls=%async_computation.2 | async-start | bytes 2097152 | tf_op jit(solution)/shard_map/psum | solution.py:95
  438.3 15.6 %collective-permute-start.2 = (bf16[256,2048]{1,0:T(8,128)(2,1)}, bf16[256,2048]{1,0:T(8,128)(2,1)S(1)}, u32[]{:S(2)}, u32[]{:S(2)}) collective-permute-start(bf16[256,2048]{1,0:T(8,128)(2,1)} %all-reduce.7.cloned.1.call-done), channel_id=1, source_target_pairs={{0,16},{16,0},{32,48},{48,32},{64,80},{80,64},{96,112},{112,96},{1... | collective-permute-start | bytes 3145736 | tf_op jit(solution)/shard_map/ppermute | solution.py:10
  451.7 80.4 %copy-start.15 = (f32[1,64,64]{2,1,0:T(8,128)}, f32[1,64,64]{2,1,0:T(8,128)S(1)}, u32[]{:S(2)}) copy-start(f32[1,64,64]{2,1,0:T(8,128)S(1)} %fusion.26) | copy-start | bytes 49156
  454.8 76.2 %copy-start.7 = (bf16[8,2048]{1,0:T(8,128)(2,1)}, bf16[8,2048]{1,0:T(8,128)(2,1)S(1)}, u32[]{:S(2)}) copy-start(bf16[8,2048]{1,0:T(8,128)(2,1)S(1)} %fusion.77) | copy-start | bytes 98308
  454.8 4.1 collective-permute-start.3
  458.9 72.1 %copy-start.12 = (bf16[1,2048,192]{1,2,0:T(8,128)(2,1)S(1)}, bf16[1,2048,192]{1,2,0:T(8,128)(2,1)}, u32[]{:S(2)}) copy-start(bf16[1,2048,192]{1,2,0:T(8,128)(2,1)} %param.15) | copy-start | bytes 2359300
  458.9 39.7 %collective-permute-start.4 = (bf16[8,2048]{1,0:T(8,128)(2,1)S(1)}, bf16[8,2048]{1,0:T(8,128)(2,1)S(1)}, u32[]{:S(2)}, u32[]{:S(2)}) collective-permute-start(bf16[8,2048]{1,0:T(8,128)(2,1)S(1)} %bitcast_select_fusion), channel_id=1, source_target_pairs={{0,16},{16,0},{32,48},{48,32},{64,80},{80,64},{96,112},{112,96},{1... | collective-permute-start | bytes 98312 | tf_op jit(solution)/shard_map/ppermute | solution.py:10
  535.3 345.0 %all-reduce.11.cloned.1.call-start = ((), (), s32[]{:S(2)}) async-start(), calls=%async_computation.3 | async-start | bytes 2097152 | tf_op jit(solution)/shard_map/psum | solution.py:95
  705.5 15.6 %collective-permute-start.5 = (bf16[256,2048]{1,0:T(8,128)(2,1)}, bf16[256,2048]{1,0:T(8,128)(2,1)S(1)}, u32[]{:S(2)}, u32[]{:S(2)}) collective-permute-start(bf16[256,2048]{1,0:T(8,128)(2,1)} %all-reduce.9.cloned.1.call-done), channel_id=1, source_target_pairs={{0,16},{16,0},{32,48},{48,32},{64,80},{80,64},{96,112},{112,96},{1... | collective-permute-start | bytes 3145736 | tf_op jit(solution)/shard_map/ppermute | solution.py:10
  722.8 2.0 copy-start.11
  724.8 168.5 %copy-start.6 = (bf16[256,1,192]{0,2,1:T(8,128)(2,1)S(1)}, bf16[256,1,192]{0,2,1:T(8,128)(2,1)}, u32[]{:S(2)}) copy-start(bf16[256,1,192]{0,2,1:T(8,128)(2,1)} %copy-done.5) | copy-start | bytes 294916
  724.8 169.2 %copy-start.16 = (f32[1,64,64]{2,1,0:T(8,128)S(1)}, f32[1,64,64]{2,1,0:T(8,128)}, u32[]{:S(2)}) copy-start(f32[1,64,64]{2,1,0:T(8,128)} %copy-done.15) | copy-start | bytes 49156
  880.3 15.6 %collective-permute-start.6 = (bf16[256,2048]{1,0:T(8,128)(2,1)}, bf16[256,2048]{1,0:T(8,128)(2,1)S(1)}, u32[]{:S(2)}, u32[]{:S(2)}) collective-permute-start(bf16[256,2048]{1,0:T(8,128)(2,1)} %all-reduce.11.cloned.1.call-done), channel_id=1, source_target_pairs={{0,16},{16,0},{32,48},{48,32},{64,80},{80,64},{96,112},{112,96},{1... | collective-permute-start | bytes 3145736 | tf_op jit(solution)/shard_map/ppermute | solution.py:10
  (4 other events, 4.0 us)
Sparse Core Ops, SparseCore 0:
  96.1 167.3 all-reduce.4
  284.6 153.7 all-reduce.6
  535.4 170.0 all-reduce.8
  726.4 153.7 all-reduce.10
where the time goes:
time: 905 us; the launch traced here: 904 us
  waiting for transfers between devices  654 us (72%)
  blocking collectives  140 us (15%)
  starting transfers between devices  67.8 us (7%)
  between operations  14.8 us (2%)
  matrix products  14.4 us (2%)
    psum x4, waiting for transfers between devices, total_all(): lax.psum(jnp.dot(local, weight, preferred_element_type=jnp.float32).astyp...  645 us
    all_gather x2, blocking collectives, collect_all(): lax.all_gather(values, 'tp', axis=0, tiled=True)  76.4 us
    ppermute x6, starting transfers between devices, partner_2(): return lax.ppermute(value, axis, pairs)  64.6 us
    all_gather x2, blocking collectives, collect_all(): lax.all_gather(partner, 'tp', axis=0, tiled=True)  63.5 us
  transfers between devices with their start and end apart: 11, of which 9 were waited for; matrix products, arithmetic and copies ran while one was open for 0% of the time, Pallas kernels for 0%

commit v1 on v0

--- a/solution.py
+++ b/solution.py
@@ -86,7 +86,9 @@
     def collect_all(values):
         partner = partner_2(values, "layer", 0)
         mine, other = (
-            lax.all_gather(values, "tp", axis=0, tiled=True),
+            jnp.concatenate(
+                lax.all_to_all(jnp.stack([values] * lax.axis_size("tp")), "tp", 0, 0), axis=0
+            ),
             lax.all_gather(partner, "tp", axis=0, tiled=True),
         )
         return ordered(mine, other)

time: 905 us -> 854 us (0.944)
  blocking collectives: 140 us -> 83 us
  waiting for transfers between devices: 654 us -> 640 us
  starting transfers between devices: 67.8 us -> 81.4 us
    all_gather x2 -> x0, blocking collectives: 76.4 us -> none  [collect_all(): lax.all_gather(values, 'tp', axis=0, tiled=True)]
    all_gather x2, blocking collectives: 63.5 us -> 83 us  [collect_all(): lax.all_gather(partner, 'tp', axis=0, tiled=True)]
    all_to_all x0 -> x2, starting transfers between devices: none -> 19.4 us  [collect_all(): lax.all_to_all(jnp.stack([values] * lax.axis_size('tp')), 'tp', 0, 0)]
    psum x4, waiting for transfers between devices: 645 us -> 631 us  [total_all(): lax.psum(jnp.dot(local, weight, preferred_element_type=jnp.float32).astyp...]
  transfers between devices with their start and end apart: 11 -> 13, of which waited for: 9 -> 10; matrix products, arithmetic and copies ran while one was open for 0% -> 0% of each run, Pallas kernels for 0% -> 0%
where the time goes in v1:
time: 854 us; the launch traced here: 853 us
  waiting for transfers between devices  640 us (75%)
  blocking collectives  83 us (10%)
  starting transfers between devices  81.4 us (10%)
  matrix products  16.1 us (2%)
  between operations  14.8 us (2%)
  other arithmetic  9.98 us (1%)
    psum x4, waiting for transfers between devices, total_all(): lax.psum(jnp.dot(local, weight, preferred_element_type=jnp.float32).astyp...  631 us
    all_gather x2, blocking collectives, collect_all(): lax.all_gather(partner, 'tp', axis=0, tiled=True)  83 us
    ppermute x6, starting transfers between devices, partner_2(): return lax.ppermute(value, axis, pairs)  58.7 us
    all_to_all x2, starting transfers between devices, collect_all(): lax.all_to_all(jnp.stack([values] * lax.axis_size('tp')), 'tp', 0, 0)  19.4 us
  transfers between devices with their start and end apart: 13, of which 10 were waited for; matrix products, arithmetic and copies ran while one was open for 0% of the time, Pallas kernels for 0%

profile of v1, /device:TPU:1, one launch (start us, length us, event | category | flops | bytes accessed | tf_op | source)
XLA Modules:
  0.0 852.8 jit_solution(967285610924587074)
XLA Ops:
  7.2 1.8 stack.4
  8.9 13.5 %all-to-all-start = ((bf16[16,8,2048]{2,1,0:T(8,128)(2,1)}), bf16[16,8,2048]{2,1,0:T(8,128)(2,1)}, u32[]{:S(2)}, u32[]{:S(2)}) async-start(bf16[16,8,2048]{2,1,0:T(8,128)(2,1)} %stack.4), calls=%async_computation | async-start | bytes 1048576 | tf_op jit(solution)/shard_map/all_to_all | solution.py:90
  22.5 2.9 collective-permute-start
  27.0 42.1 %all_gather.6 = bf16[128,2048]{1,0:T(8,128)(2,1)} all-gather(bf16[8,2048]{1,0:T(8,128)(2,1)S(1)} %collective-permute-done), channel_id=1, replica_groups=mesh['layer'=32,'tp'=16] {'tp'}, dimensions={0}, use_global_device_ids=true | all-gather | bytes 557056 | tf_op jit(solution)/shard_map/all_gather | solution.py:92
  70.7 1.7 fusion.14
  73.3 2.6 convolution_convert_fusion.3
  76.0 160.1 %all-reduce.5.cloned.1.call-done = bf16[256,2048]{1,0:T(8,128)(2,1)} async-done(((bf16[256,2048]{1,0:T(8,128)(2,1)}), bf16[256,2048]{1,0:T(8,128)(2,1)}) %all-reduce.5.cloned.1.call-update) | async-done | bytes 1048592 | tf_op jit(solution)/shard_map/psum | solution.py:97
  236.1 13.1 %collective-permute-start.1 = (bf16[256,2048]{1,0:T(8,128)(2,1)}, bf16[256,2048]{1,0:T(8,128)(2,1)S(1)}, u32[]{:S(2)}, u32[]{:S(2)}) collective-permute-start(bf16[256,2048]{1,0:T(8,128)(2,1)} %all-reduce.5.cloned.1.call-done), channel_id=1, source_target_pairs={{0,16},{16,0},{32,48},{48,32},{64,80},{80,64},{96,112},{112,96},{1... | collective-permute-start | bytes 3145736 | tf_op jit(solution)/shard_map/ppermute | solution.py:10
  251.7 1.8 multiply_reduce_fusion.1
  257.0 154.3 %all-reduce.7.cloned.1.call-done = bf16[256,2048]{1,0:T(8,128)(2,1)} async-done(((bf16[256,2048]{1,0:T(8,128)(2,1)}), bf16[256,2048]{1,0:T(8,128)(2,1)}) %all-reduce.7.cloned.1.call-update) | async-done | bytes 1048592 | tf_op jit(solution)/shard_map/psum | solution.py:97
  411.2 13.1 %collective-permute-start.2 = (bf16[256,2048]{1,0:T(8,128)(2,1)}, bf16[256,2048]{1,0:T(8,128)(2,1)S(1)}, u32[]{:S(2)}, u32[]{:S(2)}) collective-permute-start(bf16[256,2048]{1,0:T(8,128)(2,1)} %all-reduce.7.cloned.1.call-done), channel_id=1, source_target_pairs={{0,16},{16,0},{32,48},{48,32},{64,80},{80,64},{96,112},{112,96},{1... | collective-permute-start | bytes 3145736 | tf_op jit(solution)/shard_map/ppermute | solution.py:10
  424.4 2.5 collective-permute-done.2
  427.7 3.1 collective-permute-start.3
  432.7 6.0 all-to-all-start.1
  439.5 3.4 collective-permute-start.4
  443.8 40.8 %all_gather.7 = bf16[128,2048]{1,0:T(8,128)(2,1)} all-gather(bf16[8,2048]{1,0:T(8,128)(2,1)S(1)} %collective-permute-done.4), channel_id=1, replica_groups=mesh['layer'=32,'tp'=16] {'tp'}, dimensions={0}, use_global_device_ids=true | all-gather | bytes 557056 | tf_op jit(solution)/shard_map/all_gather | solution.py:92
  486.2 1.7 fusion.15
  488.9 2.6 convolution_convert_fusion.2
  491.6 162.4 %all-reduce.9.cloned.1.call-done = bf16[256,2048]{1,0:T(8,128)(2,1)} async-done(((bf16[256,2048]{1,0:T(8,128)(2,1)}), bf16[256,2048]{1,0:T(8,128)(2,1)}) %all-reduce.9.cloned.1.call-update) | async-done | bytes 1048592 | tf_op jit(solution)/shard_map/psum | solution.py:97
  654.0 13.1 %collective-permute-start.5 = (bf16[256,2048]{1,0:T(8,128)(2,1)}, bf16[256,2048]{1,0:T(8,128)(2,1)S(1)}, u32[]{:S(2)}, u32[]{:S(2)}) collective-permute-start(bf16[256,2048]{1,0:T(8,128)(2,1)} %all-reduce.9.cloned.1.call-done), channel_id=1, source_target_pairs={{0,16},{16,0},{32,48},{48,32},{64,80},{80,64},{96,112},{112,96},{1... | collective-permute-start | bytes 3145736 | tf_op jit(solution)/shard_map/ppermute | solution.py:10
  667.2 2.5 collective-permute-done.5
  669.6 1.8 multiply_reduce_fusion
  674.9 154.3 %all-reduce.11.cloned.1.call-done = bf16[256,2048]{1,0:T(8,128)(2,1)} async-done(((bf16[256,2048]{1,0:T(8,128)(2,1)}), bf16[256,2048]{1,0:T(8,128)(2,1)}) %all-reduce.11.cloned.1.call-update) | async-done | bytes 1048592 | tf_op jit(solution)/shard_map/psum | solution.py:97
  829.2 13.1 %collective-permute-start.6 = (bf16[256,2048]{1,0:T(8,128)(2,1)}, bf16[256,2048]{1,0:T(8,128)(2,1)S(1)}, u32[]{:S(2)}, u32[]{:S(2)}) collective-permute-start(bf16[256,2048]{1,0:T(8,128)(2,1)} %all-reduce.11.cloned.1.call-done), channel_id=1, source_target_pairs={{0,16},{16,0},{32,48},{48,32},{64,80},{80,64},{96,112},{112,96},{1... | collective-permute-start | bytes 3145736 | tf_op jit(solution)/shard_map/ppermute | solution.py:10
  (78 shorter events, 23.7 us)
Async XLA Ops:
  7.2 246.3 %copy-start = (bf16[2048,2,256]{2,1,0:T(2,128)(2,1)S(1)}, bf16[2048,2,256]{2,1,0:T(2,128)(2,1)}, u32[]{:S(2)}) copy-start(bf16[2048,2,256]{2,1,0:T(2,128)(2,1)} %param.17) | copy-start | bytes 6291460
  8.9 60.2 %all-to-all-start = ((bf16[16,8,2048]{2,1,0:T(8,128)(2,1)}), bf16[16,8,2048]{2,1,0:T(8,128)(2,1)}, u32[]{:S(2)}, u32[]{:S(2)}) async-start(bf16[16,8,2048]{2,1,0:T(8,128)(2,1)} %stack.4), calls=%async_computation | async-start | bytes 1048576 | tf_op jit(solution)/shard_map/all_to_all | solution.py:90
  22.4 213.7 %all-reduce.5.cloned.1.call-start = ((), (), s32[]{:S(2)}) async-start(), calls=%async_computation.2 | async-start | bytes 2097152 | tf_op jit(solution)/shard_map/psum | solution.py:97
  22.5 4.5 collective-permute-start
  70.7 2.0 copy-start.9
  70.7 2.4 copy-start.12
  76.0 335.2 %all-reduce.7.cloned.1.call-start = ((), (), s32[]{:S(2)}) async-start(), calls=%async_computation.3 | async-start | bytes 2097152 | tf_op jit(solution)/shard_map/psum | solution.py:97
  236.1 15.6 %collective-permute-start.1 = (bf16[256,2048]{1,0:T(8,128)(2,1)}, bf16[256,2048]{1,0:T(8,128)(2,1)S(1)}, u32[]{:S(2)}, u32[]{:S(2)}) collective-permute-start(bf16[256,2048]{1,0:T(8,128)(2,1)} %all-reduce.5.cloned.1.call-done), channel_id=1, source_target_pairs={{0,16},{16,0},{32,48},{48,32},{64,80},{80,64},{96,112},{112,96},{1... | collective-permute-start | bytes 3145736 | tf_op jit(solution)/shard_map/ppermute | solution.py:10
  255.5 176.3 %copy-start.8 = (bf16[2,8,2048]{2,1,0:T(8,128)(2,1)S(1)}, bf16[2,8,2048]{2,1,0:T(8,128)(2,1)}, u32[]{:S(2)}) copy-start(bf16[2,8,2048]{2,1,0:T(8,128)(2,1)} %param.12) | copy-start | bytes 196612
  257.0 181.7 %copy-start.4 = (bf16[256,1,192]{0,2,1:T(8,128)(2,1)S(1)}, bf16[256,1,192]{0,2,1:T(8,128)(2,1)}, u32[]{:S(2)}) copy-start(bf16[256,1,192]{0,2,1:T(8,128)(2,1)} %copy-done.3) | copy-start | bytes 294916
  257.0 181.8 %copy-start.13 = (f32[1,64,64]{2,1,0:T(8,128)S(1)}, f32[1,64,64]{2,1,0:T(8,128)}, u32[]{:S(2)}) copy-start(f32[1,64,64]{2,1,0:T(8,128)} %param.19) | copy-start | bytes 49156
  411.2 15.6 %collective-permute-start.2 = (bf16[256,2048]{1,0:T(8,128)(2,1)}, bf16[256,2048]{1,0:T(8,128)(2,1)S(1)}, u32[]{:S(2)}, u32[]{:S(2)}) collective-permute-start(bf16[256,2048]{1,0:T(8,128)(2,1)} %all-reduce.7.cloned.1.call-done), channel_id=1, source_target_pairs={{0,16},{16,0},{32,48},{48,32},{64,80},{80,64},{96,112},{112,96},{1... | collective-permute-start | bytes 3145736 | tf_op jit(solution)/shard_map/ppermute | solution.py:10
  427.7 58.2 %copy-start.7 = (bf16[8,2048]{1,0:T(8,128)(2,1)}, bf16[8,2048]{1,0:T(8,128)(2,1)S(1)}, u32[]{:S(2)}) copy-start(bf16[8,2048]{1,0:T(8,128)(2,1)S(1)} %fusion.77) | copy-start | bytes 98308
  427.7 4.1 collective-permute-start.3
  432.7 51.9 %all-to-all-start.1 = ((bf16[16,8,2048]{2,1,0:T(8,128)(2,1)}), bf16[16,8,2048]{2,1,0:T(8,128)(2,1)}, u32[]{:S(2)}, u32[]{:S(2)}) async-start(bf16[16,8,2048]{2,1,0:T(8,128)(2,1)} %stack.5), calls=%async_computation.1 | async-start | bytes 1048576 | tf_op jit(solution)/shard_map/all_to_all | solution.py:90
  438.6 215.4 %all-reduce.9.cloned.1.call-start = ((), (), s32[]{:S(2)}) async-start(), calls=%async_computation.4 | async-start | bytes 2097152 | tf_op jit(solution)/shard_map/psum | solution.py:97
  439.5 4.2 collective-permute-start.4
  486.2 2.4 copy-start.14
  491.6 337.7 %all-reduce.11.cloned.1.call-start = ((), (), s32[]{:S(2)}) async-start(), calls=%async_computation.5 | async-start | bytes 2097152 | tf_op jit(solution)/shard_map/psum | solution.py:97
  654.0 15.6 %collective-permute-start.5 = (bf16[256,2048]{1,0:T(8,128)(2,1)}, bf16[256,2048]{1,0:T(8,128)(2,1)S(1)}, u32[]{:S(2)}, u32[]{:S(2)}) collective-permute-start(bf16[256,2048]{1,0:T(8,128)(2,1)} %all-reduce.9.cloned.1.call-done), channel_id=1, source_target_pairs={{0,16},{16,0},{32,48},{48,32},{64,80},{80,64},{96,112},{112,96},{1... | collective-permute-start | bytes 3145736 | tf_op jit(solution)/shard_map/ppermute | solution.py:10
  671.4 2.0 copy-start.11
  673.4 168.9 %copy-start.6 = (bf16[256,1,192]{0,2,1:T(8,128)(2,1)S(1)}, bf16[256,1,192]{0,2,1:T(8,128)(2,1)}, u32[]{:S(2)}) copy-start(bf16[256,1,192]{0,2,1:T(8,128)(2,1)} %copy-done.5) | copy-start | bytes 294916
  673.4 169.6 %copy-start.15 = (f32[1,64,64]{2,1,0:T(8,128)S(1)}, f32[1,64,64]{2,1,0:T(8,128)}, u32[]{:S(2)}) copy-start(f32[1,64,64]{2,1,0:T(8,128)} %fusion.26) | copy-start | bytes 49156
  829.2 15.6 %collective-permute-start.6 = (bf16[256,2048]{1,0:T(8,128)(2,1)}, bf16[256,2048]{1,0:T(8,128)(2,1)S(1)}, u32[]{:S(2)}, u32[]{:S(2)}) collective-permute-start(bf16[256,2048]{1,0:T(8,128)(2,1)} %all-reduce.11.cloned.1.call-done), channel_id=1, source_target_pairs={{0,16},{16,0},{32,48},{48,32},{64,80},{80,64},{96,112},{112,96},{1... | collective-permute-start | bytes 3145736 | tf_op jit(solution)/shard_map/ppermute | solution.py:10
  (5 other events, 5.9 us)
Sparse Core Ops, SparseCore 0:
  76.1 159.9 all-reduce.4
  257.1 154.0 all-reduce.6
  491.7 162.3 all-reduce.8
  675.0 154.1 all-reduce.10
